TPU v7x, 32 devices: a whole 2x2x4 slice. The times are simulated.
32 devices in a mesh: groups: 2 (over y), seq: 4 (over z), tile: 2 (over x), chan: 2 (over core).
Axes of the slice: x: 2, y: 2, z: 4, core: 2. Of those that a mesh axis runs over, the one named last changes fastest.
Arguments:
- latents: bfloat16 [2, 7680, 384], P('tile', ('groups', 'seq'), 'chan'), parts along dimension 1, may hold values from -6 to 6
- norm_gain: float32 [384], replicated, may hold values from 0.1 to 1.9
- conv_weight: bfloat16 [3, 3, 3, 384, 384], P(None, None, None, None, 'chan'), may hold values from -0.0625 to 0.0625
- conv_bias: float32 [384], P('chan'), may hold values from -3 to 3
- upsample_weight: bfloat16 [3, 3, 384, 192], P(None, None, None, 'chan'), may hold values from -0.109375 to 0.109375
- upsample_bias: float32 [192], P('chan'), may hold values from -3 to 3
Outputs:
- decoded: bfloat16 [8, 192, 20, 384], P(None, ('groups', 'tile'), 'seq', 'chan'), parts along dimension 1
There are 2 independent parts, one for each index of `groups`. A program takes and returns all parts, laid end to end along the dimension named above; an argument that names none is the same for every part. Nothing has to cross between parts.
All inputs are finite; a program needn't handle non-finite values.
Results may differ from a plain program's by a relative error of at most 0.005.
Values may be sent and summed in bfloat16 or wider, within the bound.
No kernel may reach another device: no remote copies, remote signals or barrier semaphores. Data moves between devices by JAX's collectives and lax.ppermute only.
A program may use at most 64 MiB of HBM per device.

v0:
```python
import jax
import jax.numpy as jnp
from jax import lax
from jax.sharding import PartitionSpec as P

FRAMES = 8
ROWS_DEV = 24
COLS_DEV = 5
norm_eps = 1e-06


def extended(cells, sides, width):
    for axis, dim in sides:
        count = lax.axis_size(axis)
        ends = count - 1
        head = lax.slice_in_dim(cells, 0, width, axis=dim)
        tail = lax.slice_in_dim(cells, cells.shape[dim] - width, cells.shape[dim], axis=dim)
        cells = jnp.concatenate(
            [
                lax.ppermute(tail, axis, [(i, (i + 1) % count) for i in range(ends)]),
                cells,
                lax.ppermute(head, axis, [((i + 1) % count, i) for i in range(ends)]),
            ],
            axis=dim,
        )
    return cells


def activate(padded, norm_gain):
    values = padded.astype(jnp.float32)
    scale = lax.rsqrt(jnp.mean(values * values, axis=-1, keepdims=True) + norm_eps)
    return jax.nn.silu(values * scale * norm_gain).astype(jnp.bfloat16)


def body(latents, norm_gain, conv_weight, conv_bias, upsample_weight, upsample_bias):
    seq_count = lax.axis_size("seq")
    local_chan = conv_bias.shape[0]
    rows_src = FRAMES * ROWS_DEV // seq_count
    whole = lax.all_gather(latents[0], "chan", axis=1, tiled=True)
    arranged = whole.reshape(rows_src, seq_count, COLS_DEV, whole.shape[1])
    regrouped = lax.all_to_all(arranged, "seq", split_axis=1, concat_axis=0, tiled=True)
    full_field = regrouped.reshape(FRAMES, ROWS_DEV, COLS_DEV, whole.shape[1])
    padded = extended(full_field, (("seq", 2), ("tile", 1)), 1)
    field_own = lax.dynamic_slice_in_dim(
        full_field, lax.axis_index("chan") * local_chan, local_chan, 3
    )
    activation = activate(padded, norm_gain)
    shifted = jnp.pad(activation, ((2, 0), (0, 0), (0, 0), (0, 0)))
    conv_out = lax.conv_general_dilated(
        shifted[None],
        conv_weight,
        (1, 1, 1),
        "VALID",
        dimension_numbers=("NDHWC", "DHWIO", "NDHWC"),
        preferred_element_type=jnp.float32,
    )[0]
    middle = (field_own.astype(jnp.float32) + conv_out + conv_bias).astype(jnp.bfloat16)
    middle_rim = extended(middle, (("seq", 2), ("tile", 1)), 1)
    middle_full = lax.all_gather(middle_rim, "chan", axis=3, tiled=True)
    upsampled = jnp.repeat(jnp.repeat(middle_full, 2, axis=1), 2, axis=2)[:, 1:-1, 1:-1, :]
    image = lax.conv_general_dilated(
        upsampled,
        upsample_weight,
        (1, 1),
        "VALID",
        dimension_numbers=("NHWC", "HWIO", "NHWC"),
        preferred_element_type=jnp.float32,
    )
    image = image + upsample_bias
    out_chan = upsample_bias.shape[0]
    image = image.reshape(FRAMES, 2 * ROWS_DEV, COLS_DEV, 2, out_chan)
    image = jnp.transpose(image, (0, 1, 2, 4, 3)).reshape(
        FRAMES, 2 * ROWS_DEV, COLS_DEV, 2 * out_chan
    )
    return image.astype(jnp.bfloat16)


def solution(mesh):
    in_specs = (
        P("tile", ("groups", "seq"), "chan"),
        P(),
        P(None, None, None, None, "chan"),
        P("chan"),
        P(None, None, None, "chan"),
        P("chan"),
    )
    out_specs = P(None, ("groups", "tile"), "seq", "chan")
    return jax.shard_map(body, mesh=mesh, in_specs=in_specs, out_specs=out_specs, check_vma=False)
```

profile of v0, /device:TPU:0, one launch (start us, length us, event | category | flops | bytes accessed | tf_op | source)
XLA Modules:
  0.0 154.0 jit_solution(12144148786594133457)
XLA Ops:
  6.5 2.8 %all-gather = bf16[1,960,384]{1,2,0:T(8,128)(2,1)S(1)} all-gather(bf16[1,960,192]{1,2,0:T(8,128)(2,1)} %param.6), channel_id=2, replica_groups=mesh['groups'=2,'seq'=4,'tile'=2,'chan'=2] {'chan'}, dimensions={2}, use_global_device_ids=true | all-gather | bytes 1105920 | tf_op jit(solution)/shard_map/all_gather | solution.py:39
  9.4 0.4 copy.26
  9.7 0.3 reshape.28
  10.3 25.4 %all_to_all.15 = bf16[48,4,5,384]{3,0,2,1:T(8,128)(2,1)S(1)} all-to-all(bf16[48,4,5,384]{3,0,2,1:T(8,128)(2,1)S(1)} %copy.27), channel_id=1, replica_groups=mesh['groups'=2,'seq'=4,'tile'=2,'chan'=2] {'seq'}, dimensions={1} | all-to-all | bytes 1474560 | tf_op jit(solution)/shard_map/all_to_all | solution.py:41
  35.8 2.3 %collective-permute-start = (bf16[8,24,1,384]{3,1,0,2:T(8,128)(2,1)S(1)}, bf16[8,24,1,384]{3,1,0,2:T(8,128)(2,1)S(1)}, u32[]{:S(2)}, u32[]{:S(2)}) collective-permute-start(bf16[8,24,1,384]{3,1,0,2:T(8,128)(2,1)S(1)} %get-tuple-element.7), channel_id=1, source_target_pairs={{0,4},{4,8},{8,12},{1,5},{5,9},{9,13},{2,6},{6,10},{10,14},{3,7},{... | collective-permute-start | bytes 442376 | tf_op jit(solution)/shard_map/ppermute | solution.py:20
  38.1 1.3 collective-permute-start.1
  39.4 1.3 collective-permute-done
  40.7 4.4 %collective-permute-done.1 = bf16[8,24,1,384]{3,1,0,2:T(8,128)(2,1)S(1)} collective-permute-done((bf16[8,24,1,384]{3,1,0,2:T(8,128)(2,1)S(1)}, bf16[8,24,1,384]{3,1,0,2:T(8,128)(2,1)S(1)}, u32[]{:S(2)}, u32[]{:S(2)}) %collective-permute-start.1) | collective-permute-done | bytes 147488 | tf_op jit(solution)/shard_map/ppermute | solution.py:22
  45.3 3.4 %collective-permute-start.2 = (bf16[8,1,7,384]{3,1,0,2:T(2,128)(2,1)S(1)}, bf16[8,1,7,384]{3,1,0,2:T(2,128)(2,1)S(1)}, u32[]{:S(2)}, u32[]{:S(2)}) collective-permute-start(bf16[8,1,7,384]{3,1,0,2:T(2,128)(2,1)S(1)} %get-tuple-element.5), channel_id=1, source_target_pairs={{0,2},{1,3},{4,6},{5,7},{8,10},{9,11},{12,14},{13,15},{16,18},{17,... | collective-permute-start | bytes 129032 | tf_op jit(solution)/shard_map/ppermute | solution.py:20
  48.7 1.3 collective-permute-start.3
  50.0 0.8 collective-permute-done.2
  50.8 4.3 %collective-permute-done.3 = bf16[8,1,7,384]{3,1,0,2:T(2,128)(2,1)S(1)} collective-permute-done((bf16[8,1,7,384]{3,1,0,2:T(2,128)(2,1)S(1)}, bf16[8,1,7,384]{3,1,0,2:T(2,128)(2,1)S(1)}, u32[]{:S(2)}, u32[]{:S(2)}) %collective-permute-start.3) | collective-permute-done | bytes 43040 | tf_op jit(solution)/shard_map/ppermute | solution.py:22
  55.1 0.7 fusion.2
  55.8 1.5 fusion.9
  57.6 0.4 copy-done.3
  57.9 29.8 %fusion = f32[1,8,24,5,192]{4,0,3,2,1:T(1,128)S(1)} fusion(bf16[3,3,3,384,192]{3,4,2,1,0:T(8,128)(2,1)S(1)} %copy-done.3, bf16[1,10,26,7,384]{4,2,1,3,0:T(8,128)(2,1)S(1)} %pad_bitcast_fusion), kind=kOutput, calls=%fused_computation.2 | convolution fusion | flops 3822059520 | bytes 6116352 | tf_op jit(solution)/shard_map/conv_general_dilated | solution.py:49
  88.0 2.5 %collective-permute-start.4 = (bf16[8,24,1,192]{3,1,0,2:T(8,128)(2,1)S(1)}, bf16[8,24,1,192]{3,1,0,2:T(8,128)(2,1)S(1)}, u32[]{:S(2)}, u32[]{:S(2)}) collective-permute-start(bf16[8,24,1,192]{3,1,0,2:T(8,128)(2,1)S(1)} %get-tuple-element.11), channel_id=1, source_target_pairs={{0,4},{4,8},{8,12},{1,5},{5,9},{9,13},{2,6},{6,10},{10,14},{3,7},{... | collective-permute-start | bytes 221192 | tf_op jit(solution)/shard_map/ppermute | solution.py:20
  90.5 1.3 collective-permute-start.5
  91.8 0.9 collective-permute-done.4
  92.7 4.3 %collective-permute-done.5 = bf16[8,24,1,192]{3,1,0,2:T(8,128)(2,1)S(1)} collective-permute-done((bf16[8,24,1,192]{3,1,0,2:T(8,128)(2,1)S(1)}, bf16[8,24,1,192]{3,1,0,2:T(8,128)(2,1)S(1)}, u32[]{:S(2)}, u32[]{:S(2)}) %collective-permute-start.5) | collective-permute-done | bytes 73760 | tf_op jit(solution)/shard_map/ppermute | solution.py:22
  97.1 1.5 %collective-permute-start.6 = (bf16[8,1,7,192]{3,1,0,2:T(2,128)(2,1)S(1)}, bf16[8,1,7,192]{3,1,0,2:T(2,128)(2,1)S(1)}, u32[]{:S(2)}, u32[]{:S(2)}) collective-permute-start(bf16[8,1,7,192]{3,1,0,2:T(2,128)(2,1)S(1)} %get-tuple-element.9), channel_id=1, source_target_pairs={{0,2},{1,3},{4,6},{5,7},{8,10},{9,11},{12,14},{13,15},{16,18},{17,... | collective-permute-start | bytes 64520 | tf_op jit(solution)/shard_map/ppermute | solution.py:20
  98.7 1.3 collective-permute-start.7
  100.0 0.5 collective-permute-done.6
  100.5 4.3 %collective-permute-done.7 = bf16[8,1,7,192]{3,1,0,2:T(2,128)(2,1)S(1)} collective-permute-done((bf16[8,1,7,192]{3,1,0,2:T(2,128)(2,1)S(1)}, bf16[8,1,7,192]{3,1,0,2:T(2,128)(2,1)S(1)}, u32[]{:S(2)}, u32[]{:S(2)}) %collective-permute-start.7) | collective-permute-done | bytes 21536 | tf_op jit(solution)/shard_map/ppermute | solution.py:22
  104.8 0.5 pad_maximum_fusion.1
  105.3 3.5 %copy.33 = bf16[8,26,7,192]{1,0,2,3:T(8,128)(2,1)} copy(bf16[8,26,7,192]{3,1,0,2:T(8,128)(2,1)S(1)} %pad_maximum_fusion.1) | data formatting | bytes 1118208 | tf_op jit(solution)/shard_map/concatenate | solution.py:18
  108.8 14.2 %all-gather.3.cloned.1.call-done = bf16[8,26,7,384]{1,0,2,3:T(8,128)(2,1)} async-done(((bf16[8,26,7,192]{1,0,2,3:T(8,128)(2,1)}), bf16[8,26,7,384]{1,0,2,3:T(8,128)(2,1)}) %all-gather.3.cloned.1.call-update) | async-done | bytes 1118224 | tf_op jit(solution)/shard_map/all_gather | solution.py:59
  122.9 9.9 %copy.34 = bf16[8,26,7,384]{3,0,2,1:T(8,128)(2,1)S(1)} copy(bf16[8,26,7,384]{1,0,2,3:T(8,128)(2,1)} %all-gather.3.cloned.1.call-done) | data formatting | bytes 2236416 | tf_op jit(solution)/shard_map/all_gather | solution.py:59
  133.1 0.4 broadcast_in_dim.15
  133.7 8.0 %add_convert_fusion = bf16[8,48,10,96]{3,0,2,1:T(8,128)(2,1)} fusion(bf16[8,52,14,384]{3,0,2,1:T(8,128)(2,1)S(1)} %bitcast.30, bf16[3,3,384,96]{2,3,1,0:T(8,128)(2,1)S(1)} %copy-done, f32[96]{0:T(128)S(1)} %copy-done.4), kind=kOutput, calls=%fused_computation.12 | convolution fusion | flops 2548776960 | bytes 5874048 | tf_op jit(solution)/shard_map/conv_general_dilated | solution.py:61
  141.7 2.6 %copy.35 = bf16[8,48,5,2,96]{1,0,3,4,2:T(8,128)(2,1)S(1)} copy(bf16[8,48,5,2,96]{4,0,3,2,1:T(8,128)(2,1)} %bitcast.31) | data formatting | bytes 1474560 | tf_op jit(solution)/shard_map/convert_element_type | solution.py:75
  144.4 2.8 %copy.36 = bf16[8,48,5,192]{3,1,2,0:T(8,128)(2,1)} copy(bf16[8,48,5,192]{1,0,3,2:T(8,128)(2,1)S(1)} %bitcast.29) | data formatting | bytes 1474560 | tf_op jit(solution)/shard_map/convert_element_type | solution.py:75
  (21 shorter events, 1.6 us)
Async XLA Ops:
  6.5 126.9 %copy-start = (bf16[3,3,384,96]{2,3,1,0:T(8,128)(2,1)S(1)}, bf16[3,3,384,96]{2,3,1,0:T(8,128)(2,1)}, u32[]{:S(2)}) copy-start(bf16[3,3,384,96]{2,3,1,0:T(8,128)(2,1)} %param.10) | copy-start | bytes 1990660
  6.5 116.4 %all-gather.3.cloned.1.call-start = ((), (), s32[]{:S(2)}) async-start(), calls=%async_computation.1 | async-start | bytes 8257536 | tf_op jit(solution)/shard_map/all_gather | solution.py:59
  10.3 45.5 %copy-start.1 = (f32[384]{0:T(512)S(1)}, f32[384]{0:T(512)}, u32[]{:S(2)}) copy-start(f32[384]{0:T(512)} %param.7) | copy-start | bytes 4612
  35.8 4.9 %collective-permute-start = (bf16[8,24,1,384]{3,1,0,2:T(8,128)(2,1)S(1)}, bf16[8,24,1,384]{3,1,0,2:T(8,128)(2,1)S(1)}, u32[]{:S(2)}, u32[]{:S(2)}) collective-permute-start(bf16[8,24,1,384]{3,1,0,2:T(8,128)(2,1)S(1)} %get-tuple-element.7), channel_id=1, source_target_pairs={{0,4},{4,8},{8,12},{1,5},{5,9},{9,13},{2,6},{6,10},{10,14},{3,7},{... | collective-permute-start | bytes 442376 | tf_op jit(solution)/shard_map/ppermute | solution.py:20
  38.1 7.0 %collective-permute-start.1 = (bf16[8,24,1,384]{3,1,0,2:T(8,128)(2,1)S(1)}, bf16[8,24,1,384]{3,1,0,2:T(8,128)(2,1)S(1)}, u32[]{:S(2)}, u32[]{:S(2)}) collective-permute-start(bf16[8,24,1,384]{3,1,0,2:T(8,128)(2,1)S(1)} %get-tuple-element.8), channel_id=1, source_target_pairs={{4,0},{8,4},{12,8},{5,1},{9,5},{13,9},{6,2},{10,6},{14,10},{7,3},{... | collective-permute-start | bytes 442376 | tf_op jit(solution)/shard_map/ppermute | solution.py:22
  45.3 5.5 %collective-permute-start.2 = (bf16[8,1,7,384]{3,1,0,2:T(2,128)(2,1)S(1)}, bf16[8,1,7,384]{3,1,0,2:T(2,128)(2,1)S(1)}, u32[]{:S(2)}, u32[]{:S(2)}) collective-permute-start(bf16[8,1,7,384]{3,1,0,2:T(2,128)(2,1)S(1)} %get-tuple-element.5), channel_id=1, source_target_pairs={{0,2},{1,3},{4,6},{5,7},{8,10},{9,11},{12,14},{13,15},{16,18},{17,... | collective-permute-start | bytes 129032 | tf_op jit(solution)/shard_map/ppermute | solution.py:20
  48.7 6.4 %collective-permute-start.3 = (bf16[8,1,7,384]{3,1,0,2:T(2,128)(2,1)S(1)}, bf16[8,1,7,384]{3,1,0,2:T(2,128)(2,1)S(1)}, u32[]{:S(2)}, u32[]{:S(2)}) collective-permute-start(bf16[8,1,7,384]{3,1,0,2:T(2,128)(2,1)S(1)} %get-tuple-element.6), channel_id=1, source_target_pairs={{2,0},{3,1},{6,4},{7,5},{10,8},{11,9},{14,12},{15,13},{18,16},{19,... | collective-permute-start | bytes 129032 | tf_op jit(solution)/shard_map/ppermute | solution.py:22
  55.8 2.1 %copy-start.3 = (bf16[3,3,3,384,192]{3,4,2,1,0:T(8,128)(2,1)S(1)}, bf16[3,3,3,384,192]{3,4,2,1,0:T(8,128)(2,1)}, u32[]{:S(2)}) copy-start(bf16[3,3,3,384,192]{3,4,2,1,0:T(8,128)(2,1)} %param.8) | copy-start | bytes 11943940
  57.9 29.8 %copy-start.2 = (f32[192]{0:T(256)S(1)}, f32[192]{0:T(256)}, u32[]{:S(2)}) copy-start(f32[192]{0:T(256)} %param.9) | copy-start | bytes 2308
  88.0 4.7 %collective-permute-start.4 = (bf16[8,24,1,192]{3,1,0,2:T(8,128)(2,1)S(1)}, bf16[8,24,1,192]{3,1,0,2:T(8,128)(2,1)S(1)}, u32[]{:S(2)}, u32[]{:S(2)}) collective-permute-start(bf16[8,24,1,192]{3,1,0,2:T(8,128)(2,1)S(1)} %get-tuple-element.11), channel_id=1, source_target_pairs={{0,4},{4,8},{8,12},{1,5},{5,9},{9,13},{2,6},{6,10},{10,14},{3,7},{... | collective-permute-start | bytes 221192 | tf_op jit(solution)/shard_map/ppermute | solution.py:20
  90.5 6.5 %collective-permute-start.5 = (bf16[8,24,1,192]{3,1,0,2:T(8,128)(2,1)S(1)}, bf16[8,24,1,192]{3,1,0,2:T(8,128)(2,1)S(1)}, u32[]{:S(2)}, u32[]{:S(2)}) collective-permute-start(bf16[8,24,1,192]{3,1,0,2:T(8,128)(2,1)S(1)} %get-tuple-element.12), channel_id=1, source_target_pairs={{4,0},{8,4},{12,8},{5,1},{9,5},{13,9},{6,2},{10,6},{14,10},{7,3},{... | collective-permute-start | bytes 221192 | tf_op jit(solution)/shard_map/ppermute | solution.py:22
  97.1 3.4 %collective-permute-start.6 = (bf16[8,1,7,192]{3,1,0,2:T(2,128)(2,1)S(1)}, bf16[8,1,7,192]{3,1,0,2:T(2,128)(2,1)S(1)}, u32[]{:S(2)}, u32[]{:S(2)}) collective-permute-start(bf16[8,1,7,192]{3,1,0,2:T(2,128)(2,1)S(1)} %get-tuple-element.9), channel_id=1, source_target_pairs={{0,2},{1,3},{4,6},{5,7},{8,10},{9,11},{12,14},{13,15},{16,18},{17,... | collective-permute-start | bytes 64520 | tf_op jit(solution)/shard_map/ppermute | solution.py:20
  98.7 6.1 %collective-permute-start.7 = (bf16[8,1,7,192]{3,1,0,2:T(2,128)(2,1)S(1)}, bf16[8,1,7,192]{3,1,0,2:T(2,128)(2,1)S(1)}, u32[]{:S(2)}, u32[]{:S(2)}) collective-permute-start(bf16[8,1,7,192]{3,1,0,2:T(2,128)(2,1)S(1)} %get-tuple-element.10), channel_id=1, source_target_pairs={{2,0},{3,1},{6,4},{7,5},{10,8},{11,9},{14,12},{15,13},{18,16},{19,... | collective-permute-start | bytes 64520 | tf_op jit(solution)/shard_map/ppermute | solution.py:22
  133.1 0.7 copy-start.4
Sparse Core Ops, SparseCore 0:
  108.9 13.9 all-gather.2
where the time goes:
time: 154 us
  matrix products  37.8 us (25%)
  waiting for transfers between devices  35 us (23%)
  blocking collectives  28.2 us (18%)
  local copies, waits for them, and re-layouts  21.3 us (14%)
  starting transfers between devices  14.8 us (10%)
  between operations  13.6 us (9%)
  other arithmetic  3.28 us (2%)
    conv_general_dilated x1, matrix products, body(): lax.conv_general_dilated(shifted[None], conv_weight, (1, 1, 1), 'VALID',...  29.8 us
    all_to_all x1, blocking collectives, body(): lax.all_to_all(arranged, 'seq', split_axis=1, concat_axis=0, tiled=True)  25.4 us
    ppermute x4, waiting for transfers between devices, extended(): lax.ppermute(head, axis, [((i + 1) % count, i) for i in range(ends)])  17.3 us
    all_gather x1, waiting for transfers between devices, body(): middle_full = lax.all_gather(middle_rim, 'chan', axis=3, tiled=True)  14.2 us
    all_gather x1, local copies, waits for them, and re-layouts, body(): middle_full = lax.all_gather(middle_rim, 'chan', axis=3, tiled=True)  9.9 us
    ppermute x4, starting transfers between devices, extended(): lax.ppermute(tail, axis, [(i, (i + 1) % count) for i in range(ends)])  9.67 us
    conv_general_dilated x1, matrix products, body(): lax.conv_general_dilated(upsampled, upsample_weight, (1, 1), 'VALID', dim...  8.02 us
    convert_element_type x2, local copies, waits for them, and re-layouts, body(): return image.astype(jnp.bfloat16)  5.44 us
  transfers between devices with their start and end apart: 9, of which 9 were waited for; matrix products, arithmetic and copies ran while one was open for 0% of the time, Pallas kernels for 0%

commit v1 on v0

--- a/solution.py
+++ b/solution.py
@@ -38,7 +38,12 @@
     rows_src = FRAMES * ROWS_DEV // seq_count
     whole = lax.all_gather(latents[0], "chan", axis=1, tiled=True)
     arranged = whole.reshape(rows_src, seq_count, COLS_DEV, whole.shape[1])
-    regrouped = lax.all_to_all(arranged, "seq", split_axis=1, concat_axis=0, tiled=True)
+    regrouped = jnp.concatenate(
+        lax.all_to_all(
+            jnp.stack(jnp.split(arranged, lax.axis_size("seq"), 1), axis=0), "seq", 0, 0
+        ),
+        0,
+    )
     full_field = regrouped.reshape(FRAMES, ROWS_DEV, COLS_DEV, whole.shape[1])
     padded = extended(full_field, (("seq", 2), ("tile", 1)), 1)
     field_own = lax.dynamic_slice_in_dim(

time: 154 us -> 157 us (1.019)
  matrix products: 37.8 us -> 35.1 us
  waiting for transfers between devices: 35 us -> 37.5 us
    conv_general_dilated x1, matrix products: 29.8 us -> 27 us  [body(): lax.conv_general_dilated(shifted[None], conv_weight, (1, 1, 1), 'VALID',...]
    ppermute x4, waiting for transfers between devices: 3.52 us -> 6.25 us  [extended(): lax.ppermute(tail, axis, [(i, (i + 1) % count) for i in range(ends)])]
where the time goes in v1:
time: 157 us; the launch traced here: 156 us
  waiting for transfers between devices  37.5 us (24%)
  matrix products  35.1 us (22%)
  blocking collectives  28.2 us (18%)
  local copies, waits for them, and re-layouts  21.4 us (14%)
  starting transfers between devices  15.9 us (10%)
  between operations  13.6 us (9%)
  other arithmetic  4.72 us (3%)
    conv_general_dilated x1, matrix products, body(): lax.conv_general_dilated(shifted[None], conv_weight, (1, 1, 1), 'VALID',...  27 us
    all_to_all x1, blocking collectives, body(): lax.all_to_all(jnp.stack(jnp.split(arranged, lax.axis_size('seq'), 1), ax...  25.4 us
    ppermute x4, waiting for transfers between devices, extended(): lax.ppermute(head, axis, [((i + 1) % count, i) for i in range(ends)])  17 us
    all_gather x1, waiting for transfers between devices, body(): middle_full = lax.all_gather(middle_rim, 'chan', axis=3, tiled=True)  14.2 us
    ppermute x4, starting transfers between devices, extended(): lax.ppermute(tail, axis, [(i, (i + 1) % count) for i in range(ends)])  10.7 us
    all_gather x1, local copies, waits for them, and re-layouts, body(): middle_full = lax.all_gather(middle_rim, 'chan', axis=3, tiled=True)  9.9 us
    conv_general_dilated x1, matrix products, body(): lax.conv_general_dilated(upsampled, upsample_weight, (1, 1), 'VALID', dim...  8.02 us
    ppermute x4, waiting for transfers between devices, extended(): lax.ppermute(tail, axis, [(i, (i + 1) % count) for i in range(ends)])  6.25 us
  transfers between devices with their start and end apart: 9, of which 9 were waited for; matrix products, arithmetic and copies ran while one was open for 0% of the time, Pallas kernels for 0%

profile of v1, /device:TPU:0, one launch (start us, length us, event | category | flops | bytes accessed | tf_op | source)
XLA Modules:
  0.0 156.4 jit_solution(91435738804328449)
XLA Ops:
  6.5 2.8 %all-gather = bf16[1,960,384]{1,2,0:T(8,128)(2,1)S(1)} all-gather(bf16[1,960,192]{1,2,0:T(8,128)(2,1)} %param.6), channel_id=2, replica_groups=mesh['groups'=2,'seq'=4,'tile'=2,'chan'=2] {'chan'}, dimensions={2}, use_global_device_ids=true | all-gather | bytes 1105920 | tf_op jit(solution)/shard_map/all_gather | solution.py:39
  9.4 0.4 copy.23
  10.2 0.4 pad_maximum_fusion.1
  10.6 25.4 %all_to_all.5 = bf16[4,48,1,5,384]{4,1,3,2,0:T(8,128)(2,1)S(1)} all-to-all(bf16[4,48,1,5,384]{4,1,3,2,0:T(8,128)(2,1)S(1)} %copy.27), channel_id=1, replica_groups=mesh['groups'=2,'seq'=4,'tile'=2,'chan'=2] {'seq'}, dimensions={0} | all-to-all | bytes 1474560 | tf_op jit(solution)/shard_map/all_to_all | solution.py:42
  36.3 0.4 fusion.12
  36.7 2.3 %collective-permute-start = (bf16[8,24,1,384]{3,2,1,0:T(2,128)(2,1)S(1)}, bf16[8,24,1,384]{3,2,1,0:T(2,128)(2,1)S(1)}, u32[]{:S(2)}, u32[]{:S(2)}) collective-permute-start(bf16[8,24,1,384]{3,2,1,0:T(2,128)(2,1)S(1)} %get-tuple-element.9), channel_id=1, source_target_pairs={{0,4},{4,8},{8,12},{1,5},{5,9},{9,13},{2,6},{6,10},{10,14},{3,7},{... | collective-permute-start | bytes 442376 | tf_op jit(solution)/shard_map/ppermute | solution.py:20
  39.0 1.3 collective-permute-start.1
  40.3 3.7 %collective-permute-done = bf16[8,24,1,384]{3,2,1,0:T(2,128)(2,1)S(1)} collective-permute-done((bf16[8,24,1,384]{3,2,1,0:T(2,128)(2,1)S(1)}, bf16[8,24,1,384]{3,2,1,0:T(2,128)(2,1)S(1)}, u32[]{:S(2)}, u32[]{:S(2)}) %collective-permute-start) | collective-permute-done | bytes 147488 | tf_op jit(solution)/shard_map/ppermute | solution.py:20
  44.0 4.1 %collective-permute-done.1 = bf16[8,24,1,384]{3,2,1,0:T(2,128)(2,1)S(1)} collective-permute-done((bf16[8,24,1,384]{3,2,1,0:T(2,128)(2,1)S(1)}, bf16[8,24,1,384]{3,2,1,0:T(2,128)(2,1)S(1)}, u32[]{:S(2)}, u32[]{:S(2)}) %collective-permute-start.1) | collective-permute-done | bytes 147488 | tf_op jit(solution)/shard_map/ppermute | solution.py:22
  48.2 3.4 %collective-permute-start.2 = (bf16[8,1,7,384]{3,2,1,0:T(8,128)(2,1)S(1)}, bf16[8,1,7,384]{3,2,1,0:T(8,128)(2,1)S(1)}, u32[]{:S(2)}, u32[]{:S(2)}) collective-permute-start(bf16[8,1,7,384]{3,2,1,0:T(8,128)(2,1)S(1)} %get-tuple-element.5), channel_id=1, source_target_pairs={{0,2},{1,3},{4,6},{5,7},{8,10},{9,11},{12,14},{13,15},{16,18},{17,... | collective-permute-start | bytes 129032 | tf_op jit(solution)/shard_map/ppermute | solution.py:20
  51.6 1.3 collective-permute-start.3
  52.9 0.4 collective-permute-done.2
  53.3 4.3 %collective-permute-done.3 = bf16[8,1,7,384]{3,2,1,0:T(8,128)(2,1)S(1)} collective-permute-done((bf16[8,1,7,384]{3,2,1,0:T(8,128)(2,1)S(1)}, bf16[8,1,7,384]{3,2,1,0:T(8,128)(2,1)S(1)}, u32[]{:S(2)}, u32[]{:S(2)}) %collective-permute-start.3) | collective-permute-done | bytes 43040 | tf_op jit(solution)/shard_map/ppermute | solution.py:22
  57.6 1.2 fusion.2
  58.9 1.7 %fusion.9 = bf16[8,26,7,384]{3,2,1,0:T(8,128)(2,1)S(1)} fusion(f32[384]{0:T(512)S(1)} %copy-done.1, f32[8,26,7]{2,1,0:T(8,128)S(1)} %add_rsqrt_fusion, bf16[8,1,7,384]{3,2,1,0:T(8,128)(2,1)S(1)} %collective-permute-done.3, bf16[8,24,1,384]{3,2,1,0:T(2,128)(2,1)S(1)} %collective-permute-done.1, bf16[8,24,5,384]{3,2,1,0:T(8,128)(2,1)S(1)} %bitcast.36, ...), kind=kLoop, calls=%fused_computation.11 | loop fusion | flops 9504768 | bytes 2243776 | tf_op jit(solution)/shard_map/convert_element_type | solution.py:32
  61.0 27.0 %fusion = f32[1,8,24,5,192]{4,0,3,2,1:T(1,128)S(1)} fusion(bf16[3,3,3,384,192]{3,4,2,1,0:T(8,128)(2,1)S(1)} %copy-done.3, bf16[1,10,26,7,384]{4,3,2,1,0:T(8,128)(2,1)S(1)} %pad_bitcast_fusion), kind=kOutput, calls=%fused_computation.2 | convolution fusion | flops 3822059520 | bytes 6116352 | tf_op jit(solution)/shard_map/conv_general_dilated | solution.py:54
  88.1 0.5 fusion.11
  88.9 3.5 %collective-permute-start.4 = (bf16[8,24,1,192]{3,2,1,0:T(2,128)(2,1)S(1)}, bf16[8,24,1,192]{3,2,1,0:T(2,128)(2,1)S(1)}, u32[]{:S(2)}, u32[]{:S(2)}) collective-permute-start(bf16[8,24,1,192]{3,2,1,0:T(2,128)(2,1)S(1)} %get-tuple-element.15), channel_id=1, source_target_pairs={{0,4},{4,8},{8,12},{1,5},{5,9},{9,13},{2,6},{6,10},{10,14},{3,7},{... | collective-permute-start | bytes 221192 | tf_op jit(solution)/shard_map/ppermute | solution.py:20
  92.3 1.3 collective-permute-start.5
  93.6 1.9 %collective-permute-done.4 = bf16[8,24,1,192]{3,2,1,0:T(2,128)(2,1)S(1)} collective-permute-done((bf16[8,24,1,192]{3,2,1,0:T(2,128)(2,1)S(1)}, bf16[8,24,1,192]{3,2,1,0:T(2,128)(2,1)S(1)}, u32[]{:S(2)}, u32[]{:S(2)}) %collective-permute-start.4) | collective-permute-done | bytes 73760 | tf_op jit(solution)/shard_map/ppermute | solution.py:20
  95.5 4.4 %collective-permute-done.5 = bf16[8,24,1,192]{3,2,1,0:T(2,128)(2,1)S(1)} collective-permute-done((bf16[8,24,1,192]{3,2,1,0:T(2,128)(2,1)S(1)}, bf16[8,24,1,192]{3,2,1,0:T(2,128)(2,1)S(1)}, u32[]{:S(2)}, u32[]{:S(2)}) %collective-permute-start.5) | collective-permute-done | bytes 73760 | tf_op jit(solution)/shard_map/ppermute | solution.py:22
  100.0 1.6 %collective-permute-start.6 = (bf16[8,1,7,192]{3,2,1,0:T(8,128)(2,1)S(1)}, bf16[8,1,7,192]{3,2,1,0:T(8,128)(2,1)S(1)}, u32[]{:S(2)}, u32[]{:S(2)}) collective-permute-start(bf16[8,1,7,192]{3,2,1,0:T(8,128)(2,1)S(1)} %get-tuple-element.7), channel_id=1, source_target_pairs={{0,2},{1,3},{4,6},{5,7},{8,10},{9,11},{12,14},{13,15},{16,18},{17,... | collective-permute-start | bytes 64520 | tf_op jit(solution)/shard_map/ppermute | solution.py:20
  101.6 1.3 collective-permute-start.7
  103.1 4.2 %collective-permute-done.7 = bf16[8,1,7,192]{3,2,1,0:T(8,128)(2,1)S(1)} collective-permute-done((bf16[8,1,7,192]{3,2,1,0:T(8,128)(2,1)S(1)}, bf16[8,1,7,192]{3,2,1,0:T(8,128)(2,1)S(1)}, u32[]{:S(2)}, u32[]{:S(2)}) %collective-permute-start.7) | collective-permute-done | bytes 21536 | tf_op jit(solution)/shard_map/ppermute | solution.py:22
  107.4 0.7 pad_maximum_fusion.2
  108.1 3.0 %copy.32 = bf16[8,26,7,192]{1,0,2,3:T(8,128)(2,1)} copy(bf16[8,26,7,192]{3,2,1,0:T(8,128)(2,1)S(1)} %pad_maximum_fusion.2) | data formatting | bytes 1118208 | tf_op jit(solution)/shard_map/concatenate | solution.py:18
  111.1 14.2 %all-gather.3.cloned.1.call-done = bf16[8,26,7,384]{1,0,2,3:T(8,128)(2,1)} async-done(((bf16[8,26,7,192]{1,0,2,3:T(8,128)(2,1)}), bf16[8,26,7,384]{1,0,2,3:T(8,128)(2,1)}) %all-gather.3.cloned.1.call-update) | async-done | bytes 1118224 | tf_op jit(solution)/shard_map/all_gather | solution.py:64
  125.3 9.9 %copy.33 = bf16[8,26,7,384]{3,0,2,1:T(8,128)(2,1)S(1)} copy(bf16[8,26,7,384]{1,0,2,3:T(8,128)(2,1)} %all-gather.3.cloned.1.call-done) | data formatting | bytes 2236416 | tf_op jit(solution)/shard_map/all_gather | solution.py:64
  135.4 0.4 broadcast_in_dim.15
  136.1 8.0 %add_convert_fusion = bf16[8,48,10,96]{3,0,2,1:T(8,128)(2,1)} fusion(bf16[8,52,14,384]{3,0,2,1:T(8,128)(2,1)S(1)} %bitcast.40, bf16[3,3,384,96]{2,3,1,0:T(8,128)(2,1)S(1)} %copy-done, f32[96]{0:T(128)S(1)} %copy-done.4), kind=kOutput, calls=%fused_computation.12 | convolution fusion | flops 2548776960 | bytes 5874048 | tf_op jit(solution)/shard_map/conv_general_dilated | solution.py:66
  144.1 2.6 %copy.34 = bf16[8,48,5,2,96]{1,0,3,4,2:T(8,128)(2,1)S(1)} copy(bf16[8,48,5,2,96]{4,0,3,2,1:T(8,128)(2,1)} %bitcast.41) | data formatting | bytes 1474560 | tf_op jit(solution)/shard_map/convert_element_type | solution.py:80
  146.7 2.8 %copy.35 = bf16[8,48,5,192]{3,1,2,0:T(8,128)(2,1)} copy(bf16[8,48,5,192]{1,0,3,2:T(8,128)(2,1)S(1)} %bitcast.39) | data formatting | bytes 1474560 | tf_op jit(solution)/shard_map/convert_element_type | solution.py:80
  (23 shorter events, 2.4 us)
Async XLA Ops:
  6.5 129.3 %copy-start = (bf16[3,3,384,96]{2,3,1,0:T(8,128)(2,1)S(1)}, bf16[3,3,384,96]{2,3,1,0:T(8,128)(2,1)}, u32[]{:S(2)}) copy-start(bf16[3,3,384,96]{2,3,1,0:T(8,128)(2,1)} %param.10) | copy-start | bytes 1990660
  6.5 118.8 %all-gather.3.cloned.1.call-start = ((), (), s32[]{:S(2)}) async-start(), calls=%async_computation.1 | async-start | bytes 8257536 | tf_op jit(solution)/shard_map/all_gather | solution.py:64
  36.7 7.3 %collective-permute-start = (bf16[8,24,1,384]{3,2,1,0:T(2,128)(2,1)S(1)}, bf16[8,24,1,384]{3,2,1,0:T(2,128)(2,1)S(1)}, u32[]{:S(2)}, u32[]{:S(2)}) collective-permute-start(bf16[8,24,1,384]{3,2,1,0:T(2,128)(2,1)S(1)} %get-tuple-element.9), channel_id=1, source_target_pairs={{0,4},{4,8},{8,12},{1,5},{5,9},{9,13},{2,6},{6,10},{10,14},{3,7},{... | collective-permute-start | bytes 442376 | tf_op jit(solution)/shard_map/ppermute | solution.py:20
  39.0 19.9 %copy-start.1 = (f32[384]{0:T(512)S(1)}, f32[384]{0:T(512)}, u32[]{:S(2)}) copy-start(f32[384]{0:T(512)} %param.7) | copy-start | bytes 4612
  39.0 9.1 %collective-permute-start.1 = (bf16[8,24,1,384]{3,2,1,0:T(2,128)(2,1)S(1)}, bf16[8,24,1,384]{3,2,1,0:T(2,128)(2,1)S(1)}, u32[]{:S(2)}, u32[]{:S(2)}) collective-permute-start(bf16[8,24,1,384]{3,2,1,0:T(2,128)(2,1)S(1)} %get-tuple-element.10), channel_id=1, source_target_pairs={{4,0},{8,4},{12,8},{5,1},{9,5},{13,9},{6,2},{10,6},{14,10},{7,3},{... | collective-permute-start | bytes 442376 | tf_op jit(solution)/shard_map/ppermute | solution.py:22
  48.2 5.1 %collective-permute-start.2 = (bf16[8,1,7,384]{3,2,1,0:T(8,128)(2,1)S(1)}, bf16[8,1,7,384]{3,2,1,0:T(8,128)(2,1)S(1)}, u32[]{:S(2)}, u32[]{:S(2)}) collective-permute-start(bf16[8,1,7,384]{3,2,1,0:T(8,128)(2,1)S(1)} %get-tuple-element.5), channel_id=1, source_target_pairs={{0,2},{1,3},{4,6},{5,7},{8,10},{9,11},{12,14},{13,15},{16,18},{17,... | collective-permute-start | bytes 129032 | tf_op jit(solution)/shard_map/ppermute | solution.py:20
  51.6 6.0 %collective-permute-start.3 = (bf16[8,1,7,384]{3,2,1,0:T(8,128)(2,1)S(1)}, bf16[8,1,7,384]{3,2,1,0:T(8,128)(2,1)S(1)}, u32[]{:S(2)}, u32[]{:S(2)}) collective-permute-start(bf16[8,1,7,384]{3,2,1,0:T(8,128)(2,1)S(1)} %get-tuple-element.6), channel_id=1, source_target_pairs={{2,0},{3,1},{6,4},{7,5},{10,8},{11,9},{14,12},{15,13},{18,16},{19,... | collective-permute-start | bytes 129032 | tf_op jit(solution)/shard_map/ppermute | solution.py:22
  58.9 2.1 %copy-start.3 = (bf16[3,3,3,384,192]{3,4,2,1,0:T(8,128)(2,1)S(1)}, bf16[3,3,3,384,192]{3,4,2,1,0:T(8,128)(2,1)}, u32[]{:S(2)}) copy-start(bf16[3,3,3,384,192]{3,4,2,1,0:T(8,128)(2,1)} %param.8) | copy-start | bytes 11943940
  61.0 27.0 %copy-start.2 = (f32[192]{0:T(256)S(1)}, f32[192]{0:T(256)}, u32[]{:S(2)}) copy-start(f32[192]{0:T(256)} %param.9) | copy-start | bytes 2308
  88.9 6.6 %collective-permute-start.4 = (bf16[8,24,1,192]{3,2,1,0:T(2,128)(2,1)S(1)}, bf16[8,24,1,192]{3,2,1,0:T(2,128)(2,1)S(1)}, u32[]{:S(2)}, u32[]{:S(2)}) collective-permute-start(bf16[8,24,1,192]{3,2,1,0:T(2,128)(2,1)S(1)} %get-tuple-element.15), channel_id=1, source_target_pairs={{0,4},{4,8},{8,12},{1,5},{5,9},{9,13},{2,6},{6,10},{10,14},{3,7},{... | collective-permute-start | bytes 221192 | tf_op jit(solution)/shard_map/ppermute | solution.py:20
  92.3 7.6 %collective-permute-start.5 = (bf16[8,24,1,192]{3,2,1,0:T(2,128)(2,1)S(1)}, bf16[8,24,1,192]{3,2,1,0:T(2,128)(2,1)S(1)}, u32[]{:S(2)}, u32[]{:S(2)}) collective-permute-start(bf16[8,24,1,192]{3,2,1,0:T(2,128)(2,1)S(1)} %get-tuple-element.16), channel_id=1, source_target_pairs={{4,0},{8,4},{12,8},{5,1},{9,5},{13,9},{6,2},{10,6},{14,10},{7,3},{... | collective-permute-start | bytes 221192 | tf_op jit(solution)/shard_map/ppermute | solution.py:22
  100.0 3.2 %collective-permute-start.6 = (bf16[8,1,7,192]{3,2,1,0:T(8,128)(2,1)S(1)}, bf16[8,1,7,192]{3,2,1,0:T(8,128)(2,1)S(1)}, u32[]{:S(2)}, u32[]{:S(2)}) collective-permute-start(bf16[8,1,7,192]{3,2,1,0:T(8,128)(2,1)S(1)} %get-tuple-element.7), channel_id=1, source_target_pairs={{0,2},{1,3},{4,6},{5,7},{8,10},{9,11},{12,14},{13,15},{16,18},{17,... | collective-permute-start | bytes 64520 | tf_op jit(solution)/shard_map/ppermute | solution.py:20
  101.6 5.8 %collective-permute-start.7 = (bf16[8,1,7,192]{3,2,1,0:T(8,128)(2,1)S(1)}, bf16[8,1,7,192]{3,2,1,0:T(8,128)(2,1)S(1)}, u32[]{:S(2)}, u32[]{:S(2)}) collective-permute-start(bf16[8,1,7,192]{3,2,1,0:T(8,128)(2,1)S(1)} %get-tuple-element.8), channel_id=1, source_target_pairs={{2,0},{3,1},{6,4},{7,5},{10,8},{11,9},{14,12},{15,13},{18,16},{19,... | collective-permute-start | bytes 64520 | tf_op jit(solution)/shard_map/ppermute | solution.py:22
  135.4 0.7 copy-start.4
Sparse Core Ops, SparseCore 0:
  111.2 14.0 all-gather.2
